TPU v7x, 256 devices: a whole 4x4x8 slice. The times are simulated.
256 devices in a mesh: tok: 8 (over x, core), hid: 32 (over y, z).
Axes of the slice: x: 4, y: 4, z: 8, core: 2. Of those that a mesh axis runs over, the one named last changes fastest.
Arguments:
- layer_input: bfloat16 [6144, 5120], P(('tok', 'hid')), may hold values from -6 to 6
- output_grad: bfloat16 [6144, 5120], P(('tok', 'hid')), may hold values from -6 to 6
- gate_weight: bfloat16 [5120, 8192], P(None, 'hid'), may hold values from -0.078125 to 0.078125
- up_weight: bfloat16 [5120, 8192], P(None, 'hid'), may hold values from -0.078125 to 0.078125
- down_weight: bfloat16 [8192, 5120], P('hid'), may hold values from -0.0625 to 0.0625
- block_lists: int32 [48, 32], P('tok'), may hold values from 0 to 63, as said below
- block_count: int32 [48], P('tok'), may hold values from 8 to 32, as said below
Outputs:
- input_grad: bfloat16 [6144, 5120], P(('tok', 'hid'))
- gate_grad: bfloat16 [5120, 8192], P('tok', 'hid')
- up_grad: bfloat16 [5120, 8192], P('tok', 'hid')
- down_grad: bfloat16 [8192, 5120], P('hid', 'tok')
Inputs may be any that keep to these rules, and one draw needn't show every extreme that they name: Each row of block_lists holds 32 different block numbers; entries past the tile's count are valid block numbers too and are not active. `block_count`: some tile uses all 32 slots and some tile uses 8.
All inputs are finite; a program needn't handle non-finite values.
Results may differ from a plain program's by a relative error of at most 0.015.
Values may be sent and summed in bfloat16 or wider, within the bound.
No kernel may reach another device: no remote copies, remote signals or barrier semaphores. Data moves between devices by JAX's collectives and lax.ppermute only.
A program may use at most 128 MiB of HBM per device.

v0:
```python
import math
import jax
import jax.numpy as jnp
from jax import lax
from jax.sharding import Mesh, PartitionSpec as P

BLOCK = 128
TILE = 128


def to_tiles(a):
    r, c = a.shape
    return a.reshape(r // 8, 8, c // 128, 128).transpose(0, 2, 1, 3).reshape(r * c // 128, 128)


def from_tiles(a, r, c):
    return a.reshape(r // 8, c // 128, 8, 128).transpose(0, 2, 1, 3).reshape(r, c)


def tile_activity(block_lists, block_count, local_blocks):
    in_list = jnp.arange(block_lists.shape[1])[None, :] < block_count[:, None]
    hits = (block_lists[:, :, None] == local_blocks[None, None, :]) & in_list[:, :, None]
    return jnp.any(hits, axis=1)


def unit_grads(gate_pre, up_pre, grad_hidden, unit_mask):
    sigmoid_g = jax.nn.sigmoid(gate_pre)
    silu_g = gate_pre * sigmoid_g
    hidden = (unit_mask * silu_g * up_pre).astype(jnp.bfloat16)
    grad_gate = (
        unit_mask * grad_hidden * up_pre * sigmoid_g * (1.0 + gate_pre * (1.0 - sigmoid_g))
    ).astype(jnp.bfloat16)
    grad_up = (unit_mask * grad_hidden * silu_g).astype(jnp.bfloat16)
    return (hidden, grad_gate, grad_up)


def body(layer_input, output_grad, gate_weight, up_weight, down_weight, block_lists, block_count):
    contract_last = (((1,), (1,)), ((), ()))
    contract_first = (((0,), (0,)), ((), ()))
    rows, d_model = layer_input.shape
    width = gate_weight.shape[1]
    blocks_here = width // BLOCK
    local_blocks = lax.axis_index("hid") * blocks_here + jnp.arange(blocks_here, dtype=jnp.int32)
    active = tile_activity(block_lists, block_count, local_blocks)
    tok_rows = rows * lax.axis_size("hid")
    inputs_full = from_tiles(
        lax.all_gather(to_tiles(layer_input), "hid", axis=0, tiled=True), tok_rows, d_model
    )
    grads_full = from_tiles(
        lax.all_gather(to_tiles(output_grad), "hid", axis=0, tiled=True), tok_rows, d_model
    )
    tiles_here = tok_rows // TILE
    unit_mask = jnp.broadcast_to(
        active.astype(jnp.float32)[:, None, :, None], (tiles_here, TILE, blocks_here, BLOCK)
    ).reshape(tok_rows, width)
    gate_pre = jnp.dot(inputs_full, gate_weight, preferred_element_type=jnp.float32)
    up_pre = jnp.dot(inputs_full, up_weight, preferred_element_type=jnp.float32)
    grad_hidden = lax.dot_general(
        grads_full, down_weight, contract_last, preferred_element_type=jnp.float32
    )
    hidden, grad_gate, grad_up = unit_grads(gate_pre, up_pre, grad_hidden, unit_mask)
    total = lax.dot_general(
        grad_gate, gate_weight, contract_last, preferred_element_type=jnp.float32
    )
    partial = (
        total
        + lax.dot_general(grad_up, up_weight, contract_last, preferred_element_type=jnp.float32)
    ).astype(jnp.bfloat16)
    input_grad = from_tiles(
        lax.psum_scatter(to_tiles(partial), "hid", scatter_dimension=0, tiled=True), rows, d_model
    )
    scale = 1.0 / math.sqrt(tok_rows * lax.axis_size("tok"))
    term_gate = lax.dot_general(
        inputs_full, grad_gate, contract_first, preferred_element_type=jnp.float32
    )
    term_up = lax.dot_general(
        inputs_full, grad_up, contract_first, preferred_element_type=jnp.float32
    )
    term_down = lax.dot_general(
        grads_full, hidden, contract_first, preferred_element_type=jnp.float32
    )
    stacked = lax.psum_scatter(
        (jnp.concatenate([term_gate, term_up, term_down], axis=1) * scale).astype(jnp.bfloat16),
        "tok",
        scatter_dimension=0,
        tiled=True,
    ).astype(jnp.float32)
    gate_grad = stacked[:, :width].astype(jnp.bfloat16)
    up_grad = stacked[:, width : 2 * width].astype(jnp.bfloat16)
    down_grad = stacked[:, 2 * width :].T.astype(jnp.bfloat16)
    return (input_grad, gate_grad, up_grad, down_grad)


def solution(mesh):
    in_specs = (
        P(("tok", "hid"), None),
        P(("tok", "hid"), None),
        P(None, "hid"),
        P(None, "hid"),
        P("hid", None),
        P("tok", None),
        P("tok"),
    )
    out_specs = (P(("tok", "hid"), None), P("tok", "hid"), P("tok", "hid"), P("hid", "tok"))
    return jax.shard_map(body, mesh=mesh, in_specs=in_specs, out_specs=out_specs, check_vma=False)
```

profile of v0, /device:TPU:2, one launch (start us, length us, event | category | flops | bytes accessed | tf_op | source)
XLA Modules:
  0.0 524.6 jit_solution(17337344538193097124)
XLA Ops:
  7.2 0.0 copy-start
  7.2 0.0 all-gather.5.cloned.1.call-start
  7.2 0.7 all-gather.5.cloned.1.call-update
  7.9 0.0 all-gather.3.cloned.1.call-start
  8.0 0.7 all-gather.3.cloned.1.call-update
  8.7 0.0 reduce-scatter.7.cloned.1.call-start
  8.7 0.7 iota_compare_fusion
  9.5 0.9 and_reduce_fusion
  10.4 0.1 copy.15
  10.5 98.3 %all-gather.5.cloned.1.call-done = bf16[30720,128]{1,0:T(8,128)(2,1)} async-done(((bf16[960,128]{1,0:T(8,128)(2,1)}), bf16[30720,128]{1,0:T(8,128)(2,1)}) %all-gather.5.cloned.1.call-update) | async-done | bytes 7864336 | tf_op jit(solution)/shard_map/all_gather | solution.py:47
  108.8 0.0 slice-start
  108.8 0.0 copy-start.1
  108.8 0.0 copy-done
  108.8 0.0 slice-start.1
  108.8 5.6 %fusion.9 = f32[768,256]{1,0:T(8,128)S(1)} fusion(bf16[768,5120]{1,0:T(8,128)(2,1)} %bitcast.63, bf16[5120,256]{1,0:T(8,128)(2,1)S(1)} %copy-done), kind=kOutput, calls=%fused_computation.20 | convolution fusion | flops 2013265920 | bytes 11272192 | tf_op jit(solution)/shard_map/dot_general | solution.py:56
  114.4 0.0 slice-done
  114.4 0.0 copy-done.1
  114.4 0.7 slice-done.1
  115.1 0.0 copy-start.3
  115.1 3.1 fusion.8
  118.2 85.5 %all-gather.3.cloned.1.call-done = bf16[30720,128]{1,0:T(8,128)(2,1)} async-done(((bf16[960,128]{1,0:T(8,128)(2,1)}), bf16[30720,128]{1,0:T(8,128)(2,1)}) %all-gather.3.cloned.1.call-update) | async-done | bytes 7864336 | tf_op jit(solution)/shard_map/all_gather | solution.py:50
  203.7 0.0 slice-start.4
  203.7 0.3 broadcast_in_dim.2
  203.9 0.0 copy-done.3
  204.0 0.0 slice-start.5
  204.0 0.0 copy-start.4
  204.0 0.0 copy-start.5
  204.0 0.0 slice-start.2
  204.0 6.1 %convolution_bitcast_fusion = f32[5120,256]{0,1:T(8,128)S(1)} fusion(bf16[768,5120]{1,0:T(8,128)(2,1)} %bitcast.72, f32[768,256]{1,0:T(8,128)} %fusion.8, f32[96,8,2,128]{3,2,1,0:T(2,128)S(1)} %bitcast.76, f32[768,256]{1,0:T(8,128)S(1)} %fusion.9), kind=kOutput, calls=%fused_computation.3 | convolution fusion | flops 2014642176 | bytes 15466496 | tf_op jit(solution)/shard_map/dot_general | solution.py:79
  210.1 0.0 slice-done.4
  210.1 0.0 slice-done.5
  210.2 0.0 copy-done.4
  210.2 0.3 copy-done.5
  210.5 0.0 slice-start.3
  210.5 3.7 multiply_convert_fusion
  214.3 0.0 slice-done.2
  214.3 0.0 slice-done.3
  214.3 2.2 convolution_bitcast_fusion.1
  216.5 2.4 convolution_bitcast_fusion.2
  218.9 4.4 fusion
  223.4 10.6 %copy.18 = bf16[5120,768]{1,0:T(8,128)(2,1)} copy(bf16[5120,768]{0,1:T(8,128)(2,1)} %fusion) | data formatting | bytes 15728640
  234.0 0.0 reduce-scatter.7.cloned.1.call-update
  234.0 0.0 reduce-scatter.5.cloned.1.call-start
  234.1 0.0 copy-start.2
  234.1 7.7 %fusion.10 = f32[768,5120]{1,0:T(8,128)} fusion(bf16[768,256]{1,0:T(8,128)(2,1)S(1)} %get-tuple-element.17, bf16[5120,256]{1,0:T(8,128)(2,1)S(1)} %copy-done), kind=kOutput, calls=%fused_computation.21 | convolution fusion | flops 2013265920 | bytes 18743296 | tf_op jit(solution)/shard_map/dot_general | solution.py:62
  241.8 0.0 copy-done.2
  241.8 11.8 %add_convert_fusion = bf16[768,5120]{1,0:T(8,128)(2,1)} fusion(f32[768,5120]{1,0:T(8,128)} %fusion.10, bf16[768,256]{1,0:T(8,128)(2,1)S(1)} %get-tuple-element.16, bf16[5120,256]{1,0:T(8,128)(2,1)S(1)} %copy-done.2), kind=kOutput, calls=%fused_computation.2 | convolution fusion | flops 2021130240 | bytes 26607616 | tf_op jit(solution)/shard_map/dot_general | solution.py:67
  253.6 0.0 reduce-scatter.5.cloned.1.call-update
  253.6 27.8 %reduce-scatter.7.cloned.1.call-done = bf16[640,768]{1,0:T(8,128)(2,1)} async-done(((bf16[5120,768]{1,0:T(8,128)(2,1)}), bf16[640,768]{1,0:T(8,128)(2,1)}) %reduce-scatter.7.cloned.1.call-update) | async-done | bytes 983056
  281.4 2.1 fusion.7
  283.5 0.9 copy.22
  284.4 233.7 %reduce-scatter.5.cloned.1.call-done = bf16[960,128]{1,0:T(8,128)(2,1)} async-done(((bf16[30720,128]{1,0:T(8,128)(2,1)}), bf16[960,128]{1,0:T(8,128)(2,1)}) %reduce-scatter.5.cloned.1.call-update) | async-done | bytes 245776 | tf_op jit(solution)/shard_map/reduce_scatter | solution.py:70
  (5 shorter events, 0.0 us)
Async XLA Ops:
  7.2 101.6 %copy-start = (bf16[5120,256]{1,0:T(8,128)(2,1)S(1)}, bf16[5120,256]{1,0:T(8,128)(2,1)}, u32[]{:S(2)}) copy-start(bf16[5120,256]{1,0:T(8,128)(2,1)} %param.9) | copy-start | bytes 7864324
  7.2 101.6 %all-gather.5.cloned.1.call-start = ((), (), s32[]{:S(2)}) async-start(), calls=%async_computation.3 | async-start | bytes 8110080 | tf_op jit(solution)/shard_map/all_gather | solution.py:47
  7.9 195.8 %all-gather.3.cloned.1.call-start = ((), (), s32[]{:S(2)}) async-start(), calls=%async_computation.2 | async-start | bytes 8110080 | tf_op jit(solution)/shard_map/all_gather | solution.py:50
  8.7 272.7 %reduce-scatter.7.cloned.1.call-start = ((), (), s32[]{:S(2)}) async-start(), calls=%async_computation.5 | async-start | bytes 8847360
  108.8 5.6 %slice-start = ((s8[7864320]{0:T(1024)(128)(4,1)}), s8[4194304]{0:T(1024)(128)(4,1)S(1)}, s32[]{:S(2)}) async-start(s8[7864320]{0:T(1024)(128)(4,1)} %bitcast.64), calls=%async_computation.6 | async-start | bytes 8388608
  108.8 5.6 %copy-start.1 = (bf16[5120,256]{1,0:T(8,128)(2,1)S(1)}, bf16[5120,256]{1,0:T(8,128)(2,1)}, u32[]{:S(2)}) copy-start(bf16[5120,256]{1,0:T(8,128)(2,1)} %param.10) | copy-start | bytes 7864324
  108.8 6.3 %slice-start.1 = ((s8[7864320]{0:T(1024)(128)(4,1)}), s8[3670016]{0:T(1024)(128)(4,1)S(1)}, s32[]{:S(2)}) async-start(s8[7864320]{0:T(1024)(128)(4,1)} %bitcast.64), calls=%async_computation.7 | async-start | bytes 7340032
  115.1 88.9 %copy-start.3 = (f32[768,256]{1,0:T(8,128)}, f32[768,256]{1,0:T(8,128)S(1)}, u32[]{:S(2)}) copy-start(f32[768,256]{1,0:T(8,128)S(1)} %fusion.9) | copy-start | bytes 2359300
  203.7 6.5 %slice-start.4 = ((s8[7864320]{0:T(1024)(128)(4,1)}), s8[4194304]{0:T(1024)(128)(4,1)S(1)}, s32[]{:S(2)}) async-start(s8[7864320]{0:T(1024)(128)(4,1)} %bitcast.73), calls=%async_computation.10 | async-start | bytes 8388608
  204.0 6.2 %slice-start.5 = ((s8[7864320]{0:T(1024)(128)(4,1)}), s8[3670016]{0:T(1024)(128)(4,1)S(1)}, s32[]{:S(2)}) async-start(s8[7864320]{0:T(1024)(128)(4,1)} %bitcast.73), calls=%async_computation.11 | async-start | bytes 7340032
  204.0 6.2 %copy-start.4 = (f32[768,256]{1,0:T(8,128)S(1)}, f32[768,256]{1,0:T(8,128)}, u32[]{:S(2)}) copy-start(f32[768,256]{1,0:T(8,128)} %fusion.8) | copy-start | bytes 2359300
  204.0 6.5 %copy-start.5 = (bf16[256,5120]{1,0:T(8,128)(2,1)S(1)}, bf16[256,5120]{1,0:T(8,128)(2,1)}, u32[]{:S(2)}) copy-start(bf16[256,5120]{1,0:T(8,128)(2,1)} %param.11) | copy-start | bytes 7864324
  204.0 10.3 %slice-start.2 = ((s8[7864320]{0:T(1024)(128)(4,1)}), s8[4194304]{0:T(1024)(128)(4,1)S(1)}, s32[]{:S(2)}) async-start(s8[7864320]{0:T(1024)(128)(4,1)} %bitcast.67), calls=%async_computation.8 | async-start | bytes 8388608
  210.5 3.8 slice-start.3
  234.0 284.0 %reduce-scatter.5.cloned.1.call-start = ((), (), s32[]{:S(2)}) async-start(), calls=%async_computation.4 | async-start | bytes 8110080 | tf_op jit(solution)/shard_map/reduce_scatter | solution.py:70
  234.1 7.7 %copy-start.2 = (bf16[5120,256]{1,0:T(8,128)(2,1)S(1)}, bf16[5120,256]{1,0:T(8,128)(2,1)}, u32[]{:S(2)}) copy-start(bf16[5120,256]{1,0:T(8,128)(2,1)} %param.10) | copy-start | bytes 7864324
Sparse Core Ops, SparseCore 0:
  10.6 98.1 all-gather.4
  111.3 92.2 all-gather.2
  234.1 47.2 reduce-scatter.6
  285.9 232.1 reduce-scatter.4
where the time goes:
time: 525 us
  waiting for transfers between devices  447 us (85%)
  matrix products  42.7 us (8%)
  local copies, waits for them, and re-layouts  15 us (3%)
  between operations  14 us (3%)
  other arithmetic  6.04 us (1%)
    reduce_scatter x1, waiting for transfers between devices, body(): lax.psum_scatter(to_tiles(partial), 'hid', scatter_dimension=0, tiled=True)  234 us
    all_gather x1, waiting for transfers between devices, body(): lax.all_gather(to_tiles(layer_input), 'hid', axis=0, tiled=True)  98.3 us
    all_gather x1, waiting for transfers between devices, body(): lax.all_gather(to_tiles(output_grad), 'hid', axis=0, tiled=True)  85.5 us
    unnamed x5, waiting for transfers between devices  29.2 us
    unnamed x26, local copies, waits for them, and re-layouts  12.6 us
    dot_general x1, matrix products, body(): lax.dot_general(grad_up, up_weight, contract_last, preferred_element_type...  11.8 us
  transfers between devices with their start and end apart: 4, of which 4 were waited for; matrix products, arithmetic and copies ran while one was open for 6% of the time, Pallas kernels for 0%

commit v1 on v0

--- a/solution.py
+++ b/solution.py
@@ -3,6 +3,7 @@
 import jax.numpy as jnp
 from jax import lax
 from jax.sharding import Mesh, PartitionSpec as P
+from jax.lax import all_to_all, axis_size
 
 BLOCK = 128
 TILE = 128
@@ -47,7 +48,11 @@
         lax.all_gather(to_tiles(layer_input), "hid", axis=0, tiled=True), tok_rows, d_model
     )
     grads_full = from_tiles(
-        lax.all_gather(to_tiles(output_grad), "hid", axis=0, tiled=True), tok_rows, d_model
+        jnp.concatenate(
+            all_to_all(jnp.stack(axis_size("hid") * [to_tiles(output_grad)]), "hid", 0, 0), 0
+        ),
+        tok_rows,
+        d_model,
     )
     tiles_here = tok_rows // TILE
     unit_mask = jnp.broadcast_to(

time: 525 us -> 576 us (1.097)
  waiting for transfers between devices: 447 us -> 479 us
  starting transfers between devices: 0.16 us -> 11.9 us
    all_gather x1, waiting for transfers between devices: 98.3 us -> 212 us  [body(): lax.all_gather(to_tiles(layer_input), 'hid', axis=0, tiled=True)]
    all_gather x1 -> x0, waiting for transfers between devices: 85.5 us -> none  [body(): lax.all_gather(to_tiles(output_grad), 'hid', axis=0, tiled=True)]
    all_to_all x0 -> x1, starting transfers between devices: none -> 11.7 us  [body(): all_to_all(jnp.stack(axis_size('hid') * [to_tiles(output_grad)]), 'hid',...]
    another operation x0 -> x1, local copies, waits for them, and re-layouts: none -> 5.9 us  [body(): jnp.stack(axis_size('hid') * [to_tiles(output_grad)])]
    unnamed x5 -> x4, waiting for transfers between devices: 29.2 us -> 33.5 us
  transfers between devices with their start and end apart: 4 -> 4, of which waited for: 4 -> 3; matrix products, arithmetic and copies ran while one was open for 6% -> 6% of each run, Pallas kernels for 0% -> 0%
where the time goes in v1:
time: 576 us; the launch traced here: 575 us
  waiting for transfers between devices  479 us (83%)
  matrix products  44.6 us (8%)
  local copies, waits for them, and re-layouts  20.6 us (4%)
  between operations  13.9 us (2%)
  starting transfers between devices  11.9 us (2%)
    reduce_scatter x1, waiting for transfers between devices, body(): lax.psum_scatter(to_tiles(partial), 'hid', scatter_dimension=0, tiled=True)  234 us
    all_gather x1, waiting for transfers between devices, body(): lax.all_gather(to_tiles(layer_input), 'hid', axis=0, tiled=True)  212 us
    unnamed x4, waiting for transfers between devices  33.5 us
    unnamed x26, local copies, waits for them, and re-layouts  12.2 us
    all_to_all x1, starting transfers between devices, body(): all_to_all(jnp.stack(axis_size('hid') * [to_tiles(output_grad)]), 'hid',...  11.7 us
  transfers between devices with their start and end apart: 4, of which 3 were waited for; matrix products, arithmetic and copies ran while one was open for 6% of the time, Pallas kernels for 0%

profile of v1, /device:TPU:2, one launch (start us, length us, event | category | flops | bytes accessed | tf_op | source)
XLA Modules:
  0.0 575.0 jit_solution(1236392970689320825)
XLA Ops:
  7.2 0.0 copy-start
  7.2 0.0 all-gather.2.cloned.1.call-start
  7.2 0.7 all-gather.2.cloned.1.call-update
  7.9 5.9 %stack.3 = bf16[32,960,128]{2,1,0:T(8,128)(2,1)} broadcast(bf16[960,128]{1,0:T(8,128)(2,1)} %bitcast.75), dimensions={1,2} | broadcast | bytes 8110080 | tf_op jit(solution)/shard_map/stack | solution.py:52
  13.8 0.0 copy-start.7
  13.8 0.0 copy-start.5
  13.8 11.7 %all-to-all-start = ((bf16[32,960,128]{2,1,0:T(8,128)(2,1)}), bf16[32,960,128]{2,1,0:T(8,128)(2,1)}, u32[]{:S(2)}, u32[]{:S(2)}) async-start(bf16[32,960,128]{2,1,0:T(8,128)(2,1)} %stack.3), calls=%async_computation | async-start | bytes 15728640 | tf_op jit(solution)/shard_map/all_to_all | solution.py:52
  25.6 0.0 reduce-scatter.7.cloned.1.call-start
  25.6 0.0 copy-done.7
  25.6 0.1 iota_compare_fusion
  25.7 0.0 copy-done.5
  25.7 0.2 and_reduce_fusion
  25.9 0.1 copy.15
  26.0 212.1 %all-gather.2.cloned.1.call-done = bf16[30720,128]{1,0:T(8,128)(2,1)} async-done(((bf16[960,128]{1,0:T(8,128)(2,1)}), bf16[30720,128]{1,0:T(8,128)(2,1)}) %all-gather.2.cloned.1.call-update) | async-done | bytes 7864336 | tf_op jit(solution)/shard_map/all_gather | solution.py:48
  238.1 0.0 slice-start
  238.1 0.0 copy-start.1
  238.1 0.0 copy-done
  238.1 0.0 slice-start.1
  238.1 5.6 fusion.9
  243.7 0.0 slice-done
  243.7 0.0 copy-done.1
  243.7 0.7 slice-done.1
  244.4 0.0 copy-start.3
  244.4 3.2 fusion.8
  247.5 0.0 all-to-all-done
  247.5 0.3 broadcast_in_dim.2
  247.8 0.0 copy-done.3
  247.8 0.0 copy-start.4
  247.8 0.0 copy-start.6
  247.8 0.0 slice-start.2
  247.9 6.1 %convolution_bitcast_fusion = f32[5120,256]{0,1:T(8,128)S(1)} fusion(bf16[768,5120]{1,0:T(8,128)(2,1)} %bitcast.5, f32[768,256]{1,0:T(8,128)} %fusion.8, f32[96,8,2,128]{3,2,1,0:T(2,128)S(1)} %bitcast.72, f32[768,256]{1,0:T(8,128)S(1)} %fusion.9), kind=kOutput, calls=%fused_computation.3 | convolution fusion | flops 2014642176 | bytes 15466496 | tf_op jit(solution)/shard_map/dot_general | solution.py:84
  254.0 0.0 copy-done.4
  254.0 0.0 copy-done.6
  254.0 0.0 slice-start.3
  254.0 6.1 %multiply_convert_fusion = (bf16[768,256]{1,0:T(8,128)(2,1)S(1)}, bf16[768,256]{1,0:T(8,128)(2,1)S(1)}) fusion(f32[768,256]{1,0:T(8,128)} %copy-done.3, f32[768,256]{1,0:T(8,128)S(1)} %copy-done.4, bf16[768,5120]{1,0:T(8,128)(2,1)} %bitcast.5, bf16[256,5120]{1,0:T(8,128)(2,1)S(1)} %copy-done.6, f32[96,8,2,128]{3,2,1,0:T(2,128)S(1)} %bitcast.73), kind=kOutput, calls=%fused_computation.10 | convolution fusion | flops 2016018432 | bytes 13631488 | tf_op jit(solution)/shard_map/dot_general | solution.py:63
  260.1 0.0 slice-done.2
  260.1 0.0 slice-done.3
  260.1 2.2 convolution_bitcast_fusion.1
  262.4 2.4 convolution_bitcast_fusion.2
  264.8 4.4 fusion
  269.2 10.6 %copy.18 = bf16[5120,768]{1,0:T(8,128)(2,1)} copy(bf16[5120,768]{0,1:T(8,128)(2,1)} %fusion) | data formatting | bytes 15728640
  279.8 0.0 reduce-scatter.7.cloned.1.call-update
  279.8 0.0 reduce-scatter.5.cloned.1.call-start
  279.9 0.0 copy-start.2
  279.9 7.7 %fusion.10 = f32[768,5120]{1,0:T(8,128)} fusion(bf16[768,256]{1,0:T(8,128)(2,1)S(1)} %get-tuple-element.17, bf16[5120,256]{1,0:T(8,128)(2,1)S(1)} %copy-done), kind=kOutput, calls=%fused_computation.21 | convolution fusion | flops 2013265920 | bytes 18743296 | tf_op jit(solution)/shard_map/dot_general | solution.py:67
  287.7 0.0 copy-done.2
  287.7 11.2 %add_convert_fusion = bf16[768,5120]{1,0:T(8,128)(2,1)} fusion(f32[768,5120]{1,0:T(8,128)} %fusion.10, bf16[768,256]{1,0:T(8,128)(2,1)S(1)} %get-tuple-element.16, bf16[5120,256]{1,0:T(8,128)(2,1)S(1)} %copy-done.2), kind=kOutput, calls=%fused_computation.2 | convolution fusion | flops 2021130240 | bytes 26607616 | tf_op jit(solution)/shard_map/dot_general | solution.py:72
  298.9 0.0 reduce-scatter.5.cloned.1.call-update
  298.9 32.7 %reduce-scatter.7.cloned.1.call-done = bf16[640,768]{1,0:T(8,128)(2,1)} async-done(((bf16[5120,768]{1,0:T(8,128)(2,1)}), bf16[640,768]{1,0:T(8,128)(2,1)}) %reduce-scatter.7.cloned.1.call-update) | async-done | bytes 983056
  331.6 2.1 fusion.7
  333.7 0.9 copy.22
  334.6 233.9 %reduce-scatter.5.cloned.1.call-done = bf16[960,128]{1,0:T(8,128)(2,1)} async-done(((bf16[30720,128]{1,0:T(8,128)(2,1)}), bf16[960,128]{1,0:T(8,128)(2,1)}) %reduce-scatter.5.cloned.1.call-update) | async-done | bytes 245776 | tf_op jit(solution)/shard_map/reduce_scatter | solution.py:75
  (4 shorter events, 0.0 us)
Async XLA Ops:
  7.2 230.9 %copy-start = (bf16[5120,256]{1,0:T(8,128)(2,1)S(1)}, bf16[5120,256]{1,0:T(8,128)(2,1)}, u32[]{:S(2)}) copy-start(bf16[5120,256]{1,0:T(8,128)(2,1)} %param.9) | copy-start | bytes 7864324
  7.2 230.9 %all-gather.2.cloned.1.call-start = ((), (), s32[]{:S(2)}) async-start(), calls=%async_computation.3 | async-start | bytes 8110080 | tf_op jit(solution)/shard_map/all_gather | solution.py:48
  13.8 11.8 %copy-start.7 = (s32[6]{0:T(128)S(1)}, s32[6]{0:T(128)}, u32[]{:S(2)}) copy-start(s32[6]{0:T(128)} %param.13) | copy-start | bytes 76
  13.8 11.9 %copy-start.5 = (s32[6,32]{1,0:T(8,128)S(1)}, s32[6,32]{1,0:T(8,128)}, u32[]{:S(2)}) copy-start(s32[6,32]{1,0:T(8,128)} %param.12) | copy-start | bytes 2308
  13.8 233.7 %all-to-all-start = ((bf16[32,960,128]{2,1,0:T(8,128)(2,1)}), bf16[32,960,128]{2,1,0:T(8,128)(2,1)}, u32[]{:S(2)}, u32[]{:S(2)}) async-start(bf16[32,960,128]{2,1,0:T(8,128)(2,1)} %stack.3), calls=%async_computation | async-start | bytes 15728640 | tf_op jit(solution)/shard_map/all_to_all | solution.py:52
  25.6 306.1 %reduce-scatter.7.cloned.1.call-start = ((), (), s32[]{:S(2)}) async-start(), calls=%async_computation.5 | async-start | bytes 8847360
  238.1 5.6 slice-start
  238.1 5.6 copy-start.1
  238.1 6.3 %slice-start.1 = ((s8[7864320]{0:T(1024)(128)(4,1)}), s8[3670016]{0:T(1024)(128)(4,1)S(1)}, s32[]{:S(2)}) async-start(s8[7864320]{0:T(1024)(128)(4,1)} %bitcast.64), calls=%async_computation.7 | async-start | bytes 7340032
  244.4 3.4 copy-start.3
  247.8 6.2 %copy-start.4 = (f32[768,256]{1,0:T(8,128)S(1)}, f32[768,256]{1,0:T(8,128)}, u32[]{:S(2)}) copy-start(f32[768,256]{1,0:T(8,128)} %fusion.8) | copy-start | bytes 2359300
  247.8 6.2 %copy-start.6 = (bf16[256,5120]{1,0:T(8,128)(2,1)S(1)}, bf16[256,5120]{1,0:T(8,128)(2,1)}, u32[]{:S(2)}) copy-start(bf16[256,5120]{1,0:T(8,128)(2,1)} %param.11) | copy-start | bytes 7864324
  247.8 12.3 %slice-start.2 = ((s8[7864320]{0:T(1024)(128)(4,1)}), s8[4194304]{0:T(1024)(128)(4,1)S(1)}, s32[]{:S(2)}) async-start(s8[7864320]{0:T(1024)(128)(4,1)} %bitcast.67), calls=%async_computation.8 | async-start | bytes 8388608
  254.0 6.1 %slice-start.3 = ((s8[7864320]{0:T(1024)(128)(4,1)}), s8[3670016]{0:T(1024)(128)(4,1)S(1)}, s32[]{:S(2)}) async-start(s8[7864320]{0:T(1024)(128)(4,1)} %bitcast.67), calls=%async_computation.9 | async-start | bytes 7340032
  279.8 288.7 %reduce-scatter.5.cloned.1.call-start = ((), (), s32[]{:S(2)}) async-start(), calls=%async_computation.4 | async-start | bytes 8110080 | tf_op jit(solution)/shard_map/reduce_scatter | solution.py:75
  279.9 7.8 %copy-start.2 = (bf16[5120,256]{1,0:T(8,128)(2,1)S(1)}, bf16[5120,256]{1,0:T(8,128)(2,1)}, u32[]{:S(2)}) copy-start(bf16[5120,256]{1,0:T(8,128)(2,1)} %param.10) | copy-start | bytes 7864324
Sparse Core Ops, SparseCore 0:
  10.6 227.4 all-gather.1
  280.0 51.6 reduce-scatter.6
  336.2 232.2 reduce-scatter.4
